TPU v7x, 32 devices: a whole 2x2x4 slice. The times are simulated.
32 devices in a mesh: samp: 16 (over z, x, core), var: 2 (over y).
Axes of the slice: x: 2, y: 2, z: 4, core: 2. Of those that a mesh axis runs over, the one named last changes fastest.
Arguments:
- genotypes: bfloat16 [16384, 12288], P('samp', 'var'), may hold values from 0 to 2, as said below
- start_q: float32 [64, 16384], P(None, 'samp'), may hold values from 0 to 1, as said below
Outputs:
- final_q: float32 [64, 16384], P(None, 'samp')
- final_p: float32 [64, 12288], P(None, 'var')
Inputs may be any that keep to these rules, and one draw needn't show every extreme that they name: `genotypes`: genotype counts, whole numbers. `start_q`: nonnegative proportions.
All inputs are finite; a program needn't handle non-finite values.
Results may differ from a plain program's by a relative error of at most 0.001.
Values sent between devices are 32-bit elements; how exact they have to be, the bound alone decides.
No kernel may reach another device: no remote copies, remote signals or barrier semaphores. Data moves between devices by JAX's collectives and lax.ppermute only.
A program may use at most 64 MiB of HBM per device.

v0:
```python
import jax
import jax.numpy as jnp
from jax import lax
from jax.sharding import PartitionSpec as P

ITERS = 2
ridge_term = 1.0


def gram_solve(gram_matrix, right_side):
    eye_matrix = jnp.eye(gram_matrix.shape[0], dtype=jnp.float32)
    factor_low = jnp.linalg.cholesky(gram_matrix + ridge_term * eye_matrix)
    return jax.scipy.linalg.cho_solve((factor_low, True), right_side)


def body(genotypes, start_q):
    halved = genotypes * jnp.asarray(0.5, dtype=genotypes.dtype)
    ancestry = start_q
    frequency = None
    for iteration in range(ITERS):
        ancestry_b = ancestry.astype(jnp.bfloat16)
        cross_part = jnp.dot(ancestry_b, halved, preferred_element_type=jnp.float32)
        gram_part = jnp.dot(ancestry, ancestry.T, precision=lax.Precision.HIGHEST)
        width = cross_part.shape[1]
        summed = lax.psum(jnp.concatenate([cross_part, gram_part], axis=1), "samp")
        frequency = gram_solve(summed[:, width:], summed[:, :width])
        freq_b = frequency.astype(jnp.bfloat16)
        sample_part = lax.dot_general(
            freq_b, halved, (((1,), (1,)), ((), ())), preferred_element_type=jnp.float32
        )
        pgram_part = jnp.dot(frequency, frequency.T, precision=lax.Precision.HIGHEST)
        sample_share = lax.psum_scatter(sample_part, "var", scatter_dimension=1, tiled=True)
        gram_p = lax.psum(pgram_part, "var")
        ancestry_share = gram_solve(gram_p, sample_share)
        ancestry = lax.all_gather(ancestry_share, "var", axis=1, tiled=True)
    return (ancestry, frequency)


def solution(mesh):
    return jax.shard_map(
        body,
        mesh=mesh,
        in_specs=(P("samp", "var"), P(None, "samp")),
        out_specs=(P(None, "samp"), P(None, "var")),
        check_vma=False,
    )
```

profile of v0, /device:TPU:0, one launch (start us, length us, event | category | flops | bytes accessed | tf_op | source)
XLA Modules:
  0.0 362.6 jit_solution(11005803779710166309)
XLA Ops:
  8.7 6.6 %fusion.8 = f32[64,6144]{0,1:T(8,128)S(1)} fusion(bf16[1024,6144]{1,0:T(8,128)(2,1)} %param.7, f32[64,1024]{1,0:T(8,128)} %param.8), kind=kOutput, calls=%fused_computation.8 | convolution fusion | flops 811663360 | bytes 14417920 | tf_op jit(solution)/shard_map/dot_general | solution.py:22
  15.3 1.9 pad_maximum_fusion
  17.4 106.9 %all-reduce.3.cloned.1.call-done = f32[64,6208]{0,1:T(8,128)} async-done(((f32[64,6208]{0,1:T(8,128)}), f32[64,6208]{0,1:T(8,128)}) %all-reduce.3.cloned.1.call-update) | async-done | bytes 1589264 | tf_op jit(solution)/shard_map/psum | solution.py:25
  125.9 5.8 %cholesky.74 = f32[64,64]{1,0:T(8,128)S(1)} custom-call(f32[64,64]{1,0:T(8,128)S(1)} %fusion.44), custom_call_target="Cholesky" | custom-call | tf_op jit(solution)/shard_map/jit(cholesky)/cholesky | solution.py:12
  133.1 4.9 %custom-call.14 = f32[1,64,64]{1,2,0:T(8,128)S(1)} custom-call(f32[1,64,64]{2,1,0:T(8,128)S(1)} %fusion.23), custom_call_target="InvertDiagBlocksLowerTriangular" | custom-call | tf_op jit(solution)/shard_map/jit(_cho_solve)/triangular_solve | solution.py:13
  138.0 5.3 %fusion.17 = f32[64,6144]{1,0:T(8,128)S(1)} fusion(f32[64,6208]{0,1:T(8,128)} %all-reduce.3.cloned.1.call-done, f32[1,64,64]{1,2,0:T(8,128)S(1)} %custom-call.14), kind=kOutput, calls=%fused_computation.17 | convolution fusion | flops 301989888 | bytes 4734976 | tf_op jit(solution)/shard_map/jit(_cho_solve)/triangular_solve | solution.py:13
  143.3 1.5 fusion.41
  146.2 9.2 %fusion.4 = f32[64,1024]{1,0:T(8,128)} fusion(bf16[1024,6144]{1,0:T(8,128)(2,1)} %param.7, f32[64,6144]{1,0:T(8,128)S(1)} %fusion.41), kind=kOutput, calls=%fused_computation.4 | convolution fusion | flops 811991040 | bytes 14417920 | tf_op jit(solution)/shard_map/dot_general | solution.py:28
  155.4 8.3 %psum.29 = f32[64,64]{0,1:T(8,128)S(1)} all-reduce(f32[64,64]{0,1:T(8,128)S(1)} %fusion.56), channel_id=1, replica_groups=mesh['samp'=16,'var'=2] {'var'}, use_global_device_ids=true, to_apply=%region_3.6 | all-reduce | flops 4096 | bytes 32768 | tf_op jit(solution)/shard_map/psum | solution.py:33
  164.1 5.8 %cholesky.85 = f32[64,64]{1,0:T(8,128)S(1)} custom-call(f32[64,64]{1,0:T(8,128)S(1)} %fusion.40), custom_call_target="Cholesky" | custom-call | tf_op jit(solution)/shard_map/jit(cholesky)/cholesky | solution.py:12
  171.3 4.9 %custom-call.15 = f32[1,64,64]{1,2,0:T(8,128)S(1)} custom-call(f32[1,64,64]{2,1,0:T(8,128)S(1)} %fusion.24), custom_call_target="InvertDiagBlocksLowerTriangular" | custom-call | tf_op jit(solution)/shard_map/jit(_cho_solve)/triangular_solve | solution.py:13
  177.7 5.6 %all_gather.6 = f32[64,1024]{1,0:T(8,128)S(1)} all-gather(f32[64,512]{1,0:T(8,128)S(1)} %fusion.36), channel_id=1, replica_groups=mesh['samp'=16,'var'=2] {'var'}, dimensions={1}, use_global_device_ids=true | all-gather | bytes 393216 | tf_op jit(solution)/shard_map/all_gather | solution.py:35
  183.8 8.0 %fusion.2 = f32[64,6144]{0,1:T(8,128)S(1)} fusion(bf16[1024,6144]{1,0:T(8,128)(2,1)} %param.7, f32[64,1024]{1,0:T(8,128)S(1)} %all_gather.6), kind=kOutput, calls=%fused_computation.2 | convolution fusion | flops 811663360 | bytes 14417920 | tf_op jit(solution)/shard_map/dot_general | solution.py:22
  191.7 1.9 pad_maximum_fusion.1
  193.7 103.0 %all-reduce.5.cloned.1.call-done = f32[64,6208]{0,1:T(8,128)} async-done(((f32[64,6208]{0,1:T(8,128)}), f32[64,6208]{0,1:T(8,128)}) %all-reduce.5.cloned.1.call-update) | async-done | bytes 1589264 | tf_op jit(solution)/shard_map/psum | solution.py:25
  298.3 5.8 %cholesky.96 = f32[64,64]{1,0:T(8,128)S(1)} custom-call(f32[64,64]{1,0:T(8,128)S(1)} %fusion.35), custom_call_target="Cholesky" | custom-call | tf_op jit(solution)/shard_map/jit(cholesky)/cholesky | solution.py:12
  305.4 4.9 %custom-call.16 = f32[1,64,64]{1,2,0:T(8,128)S(1)} custom-call(f32[1,64,64]{2,1,0:T(8,128)S(1)} %fusion.25), custom_call_target="InvertDiagBlocksLowerTriangular" | custom-call | tf_op jit(solution)/shard_map/jit(_cho_solve)/triangular_solve | solution.py:13
  310.3 5.3 %fusion.15 = f32[64,6144]{1,0:T(8,128)S(1)} fusion(f32[64,6208]{0,1:T(8,128)} %all-reduce.5.cloned.1.call-done, f32[1,64,64]{1,2,0:T(8,128)S(1)} %custom-call.16), kind=kOutput, calls=%fused_computation.15 | convolution fusion | flops 301989888 | bytes 4734976 | tf_op jit(solution)/shard_map/jit(_cho_solve)/triangular_solve | solution.py:13
  315.7 1.5 fusion.32
  318.6 9.2 %fusion = f32[64,1024]{1,0:T(8,128)} fusion(bf16[1024,6144]{1,0:T(8,128)(2,1)} %param.7, f32[64,6144]{1,0:T(8,128)S(1)} %fusion.32), kind=kOutput, calls=%fused_computation | convolution fusion | flops 811991040 | bytes 14417920 | tf_op jit(solution)/shard_map/dot_general | solution.py:28
  327.8 8.3 %psum.31 = f32[64,64]{0,1:T(8,128)S(1)} all-reduce(f32[64,64]{0,1:T(8,128)S(1)} %fusion.58), channel_id=1, replica_groups=mesh['samp'=16,'var'=2] {'var'}, use_global_device_ids=true, to_apply=%region_6.10 | all-reduce | flops 4096 | bytes 32768 | tf_op jit(solution)/shard_map/psum | solution.py:33
  336.2 5.8 %cholesky.107 = f32[64,64]{1,0:T(8,128)S(1)} custom-call(f32[64,64]{1,0:T(8,128)S(1)} %fusion.31), custom_call_target="Cholesky" | custom-call | tf_op jit(solution)/shard_map/jit(cholesky)/cholesky | solution.py:12
  343.3 4.9 %custom-call.17 = f32[1,64,64]{1,2,0:T(8,128)S(1)} custom-call(f32[1,64,64]{2,1,0:T(8,128)S(1)} %fusion.26), custom_call_target="InvertDiagBlocksLowerTriangular" | custom-call | tf_op jit(solution)/shard_map/jit(_cho_solve)/triangular_solve | solution.py:13
  349.7 5.6 %all_gather.7 = f32[64,1024]{1,0:T(8,128)S(1)} all-gather(f32[64,512]{1,0:T(8,128)S(1)} %fusion.27), channel_id=1, replica_groups=mesh['samp'=16,'var'=2] {'var'}, dimensions={1}, use_global_device_ids=true | all-gather | bytes 393216 | tf_op jit(solution)/shard_map/all_gather | solution.py:35
  (45 shorter events, 17.6 us)
Async XLA Ops:
  7.2 117.1 %all-reduce.3.cloned.1.call-start = ((), (), s32[]{:S(2)}) async-start(), calls=%async_computation.2 | async-start | bytes 6356992 | tf_op jit(solution)/shard_map/psum | solution.py:25
  17.2 159.1 %reduce-scatter.3.cloned.1.call-start = ((), (), s32[]{:S(2)}) async-start(), calls=%async_computation.3 | async-start | bytes 393216 | tf_op jit(solution)/shard_map/reduce_scatter | solution.py:32
  163.7 132.9 %all-reduce.5.cloned.1.call-start = ((), (), s32[]{:S(2)}) async-start(), calls=%async_computation.4 | async-start | bytes 6356992 | tf_op jit(solution)/shard_map/psum | solution.py:25
  193.6 154.6 %reduce-scatter.5.cloned.1.call-start = ((), (), s32[]{:S(2)}) async-start(), calls=%async_computation.5 | async-start | bytes 393216 | tf_op jit(solution)/shard_map/reduce_scatter | solution.py:32
  317.2 10.6 %copy-start = (f32[64,6144]{1,0:T(8,128)}, f32[64,6144]{1,0:T(8,128)S(1)}, u32[]{:S(2)}) copy-start(f32[64,6144]{1,0:T(8,128)S(1)} %fusion.32) | copy-start | bytes 4718596
Sparse Core Ops, SparseCore 0:
  17.3 106.9 all-reduce.2
  163.9 10.4 reduce-scatter.2
  193.8 102.8 all-reduce.4
  336.3 10.3 reduce-scatter.4
where the time goes:
time: 363 us
  waiting for transfers between devices  210 us (58%)
  other arithmetic  55.1 us (15%)
  matrix products  54.1 us (15%)
  blocking collectives  27.9 us (8%)
  between operations  14 us (4%)
    psum x2, waiting for transfers between devices, body(): summed = lax.psum(jnp.concatenate([cross_part, gram_part], axis=1), 'samp')  210 us
    another operation x12, other arithmetic, gram_solve(): factor_low = jnp.linalg.cholesky(gram_matrix + ridge_term * eye_matrix)  26.1 us
    another operation x8, other arithmetic, gram_solve(): return jax.scipy.linalg.cho_solve((factor_low, True), right_side)  22.1 us
    dot_general x2, matrix products, body(): lax.dot_general(freq_b, halved, (((1,), (1,)), ((), ())), preferred_eleme...  18.4 us
    psum x2, blocking collectives, body(): gram_p = lax.psum(pgram_part, 'var')  16.6 us
    another operation x8, matrix products, gram_solve(): return jax.scipy.linalg.cho_solve((factor_low, True), right_side)  16.6 us
    dot_general x2, matrix products, body(): cross_part = jnp.dot(ancestry_b, halved, preferred_element_type=jnp.float32)  14.5 us
    all_gather x2, blocking collectives, body(): ancestry = lax.all_gather(ancestry_share, 'var', axis=1, tiled=True)  11.3 us
  transfers between devices with their start and end apart: 4, of which 2 were waited for; matrix products, arithmetic and copies ran while one was open for 7% of the time, Pallas kernels for 0%

commit v1 on v0

--- a/solution.py
+++ b/solution.py
@@ -22,7 +22,9 @@
         cross_part = jnp.dot(ancestry_b, halved, preferred_element_type=jnp.float32)
         gram_part = jnp.dot(ancestry, ancestry.T, precision=lax.Precision.HIGHEST)
         width = cross_part.shape[1]
-        summed = lax.psum(jnp.concatenate([cross_part, gram_part], axis=1), "samp")
+        x = jnp.concatenate([cross_part, gram_part], axis=1)
+        parts = lax.all_gather(x, "samp", axis=0, tiled=False)
+        summed = parts.sum(axis=0)
         frequency = gram_solve(summed[:, width:], summed[:, :width])
         freq_b = frequency.astype(jnp.bfloat16)
         sample_part = lax.dot_general(

time: 363 us -> 424 us (1.17)
  waiting for transfers between devices: 210 us -> 264 us
  other arithmetic: 55.1 us -> 70.3 us
  matrix products: 54.1 us -> 46.1 us
    all_gather x0 -> x2, waiting for transfers between devices: none -> 264 us  [body(): parts = lax.all_gather(x, 'samp', axis=0, tiled=False)]
    psum x2 -> x0, waiting for transfers between devices: 210 us -> none  [body(): summed = lax.psum(jnp.concatenate([cross_part, gram_part], axis=1), 'samp')]
    reduce_sum x0 -> x2, other arithmetic: none -> 19.4 us  [body(): summed = parts.sum(axis=0)]
    another operation x8, matrix products: 16.6 us -> 8.94 us  [gram_solve(): return jax.scipy.linalg.cho_solve((factor_low, True), right_side)]
  transfers between devices with their start and end apart: 4 -> 4, of which waited for: 2 -> 2; matrix products, arithmetic and copies ran while one was open for 7% -> 6% of each run, Pallas kernels for 0% -> 0%
where the time goes in v1:
time: 424 us
  waiting for transfers between devices  264 us (62%)
  other arithmetic  70.3 us (17%)
  matrix products  46.1 us (11%)
  blocking collectives  27.9 us (7%)
  between operations  14.1 us (3%)
    all_gather x2, waiting for transfers between devices, body(): parts = lax.all_gather(x, 'samp', axis=0, tiled=False)  264 us
    another operation x12, other arithmetic, gram_solve(): factor_low = jnp.linalg.cholesky(gram_matrix + ridge_term * eye_matrix)  26.1 us
    another operation x8, other arithmetic, gram_solve(): return jax.scipy.linalg.cho_solve((factor_low, True), right_side)  22.1 us
    reduce_sum x2, other arithmetic, body(): summed = parts.sum(axis=0)  19.4 us
    dot_general x2, matrix products, body(): lax.dot_general(freq_b, halved, (((1,), (1,)), ((), ())), preferred_eleme...  18.4 us
    psum x2, blocking collectives, body(): gram_p = lax.psum(pgram_part, 'var')  16.6 us
    dot_general x2, matrix products, body(): cross_part = jnp.dot(ancestry_b, halved, preferred_element_type=jnp.float32)  14.2 us
    all_gather x2, blocking collectives, body(): ancestry = lax.all_gather(ancestry_share, 'var', axis=1, tiled=True)  11.3 us
  transfers between devices with their start and end apart: 4, of which 2 were waited for; matrix products, arithmetic and copies ran while one was open for 6% of the time, Pallas kernels for 0%

profile of v1, /device:TPU:0, one launch (start us, length us, event | category | flops | bytes accessed | tf_op | source)
XLA Modules:
  0.0 424.0 jit_solution(12390600945230578623)
XLA Ops:
  8.7 7.1 %fusion.8 = f32[64,6144]{1,0:T(8,128)S(1)} fusion(bf16[1024,6144]{1,0:T(8,128)(2,1)} %param.7, f32[64,1024]{1,0:T(8,128)} %param.8), kind=kOutput, calls=%fused_computation.8 | convolution fusion | flops 811663360 | bytes 14417920 | tf_op jit(solution)/shard_map/dot_general | solution.py:22
  17.2 133.8 %all-gather.5.cloned.1.call-done = f32[1024,6208]{1,0:T(8,128)} async-done(((f32[64,6208]{1,0:T(8,128)}), f32[1024,6208]{1,0:T(8,128)}) %all-gather.5.cloned.1.call-update) | async-done | bytes 25427984 | tf_op jit(solution)/shard_map/all_gather | solution.py:26
  151.0 9.7 %reduce_sum.18 = f32[64,6208]{1,0:T(8,128)S(1)} reduce(f32[16,64,6208]{2,1,0:T(8,128)} %bitcast.63, f32[]{:T(128)} %constant.47.clone.1), dimensions={0}, to_apply=%region_0.0 | reduce | flops 5959680 | bytes 27017220 | tf_op jit(solution)/shard_map/reduce_sum | solution.py:27
  160.9 5.8 %cholesky.74 = f32[64,64]{1,0:T(8,128)S(1)} custom-call(f32[64,64]{1,0:T(8,128)S(1)} %fusion.44), custom_call_target="Cholesky" | custom-call | tf_op jit(solution)/shard_map/jit(cholesky)/cholesky | solution.py:12
  168.1 4.9 %custom-call.14 = f32[1,64,64]{1,2,0:T(8,128)S(1)} custom-call(f32[1,64,64]{2,1,0:T(8,128)S(1)} %fusion.23), custom_call_target="InvertDiagBlocksLowerTriangular" | custom-call | tf_op jit(solution)/shard_map/jit(_cho_solve)/triangular_solve | solution.py:13
  173.0 1.5 fusion.17
  174.5 1.5 fusion.41
  177.4 9.2 %fusion.4 = f32[64,1024]{1,0:T(8,128)} fusion(bf16[1024,6144]{1,0:T(8,128)(2,1)} %param.7, f32[64,6144]{1,0:T(8,128)S(1)} %fusion.41), kind=kOutput, calls=%fused_computation.4 | convolution fusion | flops 811991040 | bytes 14417920 | tf_op jit(solution)/shard_map/dot_general | solution.py:30
  186.6 8.3 %psum.14 = f32[64,64]{0,1:T(8,128)S(1)} all-reduce(f32[64,64]{0,1:T(8,128)S(1)} %fusion.56), channel_id=1, replica_groups=mesh['samp'=16,'var'=2] {'var'}, use_global_device_ids=true, to_apply=%region_3.6 | all-reduce | flops 4096 | bytes 32768 | tf_op jit(solution)/shard_map/psum | solution.py:35
  195.3 5.8 %cholesky.85 = f32[64,64]{1,0:T(8,128)S(1)} custom-call(f32[64,64]{1,0:T(8,128)S(1)} %fusion.40), custom_call_target="Cholesky" | custom-call | tf_op jit(solution)/shard_map/jit(cholesky)/cholesky | solution.py:12
  202.5 4.9 %custom-call.15 = f32[1,64,64]{1,2,0:T(8,128)S(1)} custom-call(f32[1,64,64]{2,1,0:T(8,128)S(1)} %fusion.24), custom_call_target="InvertDiagBlocksLowerTriangular" | custom-call | tf_op jit(solution)/shard_map/jit(_cho_solve)/triangular_solve | solution.py:13
  208.9 5.6 %all_gather.20 = f32[64,1024]{1,0:T(8,128)S(1)} all-gather(f32[64,512]{1,0:T(8,128)S(1)} %fusion.36), channel_id=1, replica_groups=mesh['samp'=16,'var'=2] {'var'}, dimensions={1}, use_global_device_ids=true | all-gather | bytes 393216 | tf_op jit(solution)/shard_map/all_gather | solution.py:37
  214.9 7.0 %fusion.2 = f32[64,6144]{1,0:T(8,128)S(1)} fusion(bf16[1024,6144]{1,0:T(8,128)(2,1)} %param.7, f32[64,1024]{1,0:T(8,128)S(1)} %all_gather.20), kind=kOutput, calls=%fused_computation.2 | convolution fusion | flops 811663360 | bytes 14417920 | tf_op jit(solution)/shard_map/dot_general | solution.py:22
  223.3 130.2 %all-gather.7.cloned.1.call-done = f32[1024,6208]{1,0:T(8,128)} async-done(((f32[64,6208]{1,0:T(8,128)}), f32[1024,6208]{1,0:T(8,128)}) %all-gather.7.cloned.1.call-update) | async-done | bytes 25427984 | tf_op jit(solution)/shard_map/all_gather | solution.py:26
  353.5 9.7 %reduce_sum.19 = f32[64,6208]{1,0:T(8,128)S(1)} reduce(f32[16,64,6208]{2,1,0:T(8,128)} %bitcast.62, f32[]{:T(128)} %constant.47.clone.1), dimensions={0}, to_apply=%region_5.0 | reduce | flops 5959680 | bytes 27017220 | tf_op jit(solution)/shard_map/reduce_sum | solution.py:27
  363.4 5.8 %cholesky.96 = f32[64,64]{1,0:T(8,128)S(1)} custom-call(f32[64,64]{1,0:T(8,128)S(1)} %fusion.35), custom_call_target="Cholesky" | custom-call | tf_op jit(solution)/shard_map/jit(cholesky)/cholesky | solution.py:12
  370.6 4.9 %custom-call.16 = f32[1,64,64]{1,2,0:T(8,128)S(1)} custom-call(f32[1,64,64]{2,1,0:T(8,128)S(1)} %fusion.25), custom_call_target="InvertDiagBlocksLowerTriangular" | custom-call | tf_op jit(solution)/shard_map/jit(_cho_solve)/triangular_solve | solution.py:13
  375.5 1.5 fusion.15
  377.0 1.5 fusion.32
  379.9 9.2 %fusion = f32[64,1024]{1,0:T(8,128)} fusion(bf16[1024,6144]{1,0:T(8,128)(2,1)} %param.7, f32[64,6144]{1,0:T(8,128)S(1)} %fusion.32), kind=kOutput, calls=%fused_computation | convolution fusion | flops 811991040 | bytes 14417920 | tf_op jit(solution)/shard_map/dot_general | solution.py:30
  389.1 8.3 %psum.15 = f32[64,64]{0,1:T(8,128)S(1)} all-reduce(f32[64,64]{0,1:T(8,128)S(1)} %fusion.58), channel_id=1, replica_groups=mesh['samp'=16,'var'=2] {'var'}, use_global_device_ids=true, to_apply=%region_6.10 | all-reduce | flops 4096 | bytes 32768 | tf_op jit(solution)/shard_map/psum | solution.py:35
  397.6 5.8 %cholesky.107 = f32[64,64]{1,0:T(8,128)S(1)} custom-call(f32[64,64]{1,0:T(8,128)S(1)} %fusion.31), custom_call_target="Cholesky" | custom-call | tf_op jit(solution)/shard_map/jit(cholesky)/cholesky | solution.py:12
  404.7 4.9 %custom-call.17 = f32[1,64,64]{1,2,0:T(8,128)S(1)} custom-call(f32[1,64,64]{2,1,0:T(8,128)S(1)} %fusion.26), custom_call_target="InvertDiagBlocksLowerTriangular" | custom-call | tf_op jit(solution)/shard_map/jit(_cho_solve)/triangular_solve | solution.py:13
  411.1 5.6 %all_gather.23 = f32[64,1024]{1,0:T(8,128)S(1)} all-gather(f32[64,512]{1,0:T(8,128)S(1)} %fusion.27), channel_id=1, replica_groups=mesh['samp'=16,'var'=2] {'var'}, dimensions={1}, use_global_device_ids=true | all-gather | bytes 393216 | tf_op jit(solution)/shard_map/all_gather | solution.py:37
  (51 shorter events, 17.1 us)
Async XLA Ops:
  7.2 143.8 %all-gather.5.cloned.1.call-start = ((), (), s32[]{:S(2)}) async-start(), calls=%async_computation.4 | async-start | bytes 27295744 | tf_op jit(solution)/shard_map/all_gather | solution.py:26
  17.1 190.3 %reduce-scatter.3.cloned.1.call-start = ((), (), s32[]{:S(2)}) async-start(), calls=%async_computation.2 | async-start | bytes 393216 | tf_op jit(solution)/shard_map/reduce_scatter | solution.py:34
  194.9 158.6 %all-gather.7.cloned.1.call-start = ((), (), s32[]{:S(2)}) async-start(), calls=%async_computation.5 | async-start | bytes 27295744 | tf_op jit(solution)/shard_map/all_gather | solution.py:26
  223.3 186.3 %reduce-scatter.5.cloned.1.call-start = ((), (), s32[]{:S(2)}) async-start(), calls=%async_computation.3 | async-start | bytes 393216 | tf_op jit(solution)/shard_map/reduce_scatter | solution.py:34
  378.5 1.4 copy-start
Sparse Core Ops, SparseCore 0:
  17.3 133.6 all-gather.4
  195.1 11.0 reduce-scatter.2
  223.4 130.0 all-gather.6
  397.7 10.9 reduce-scatter.4
